TPU v7x, 512 devices: a whole 4x8x8 slice. The times are simulated.
512 devices in a mesh: blk: 64 (over z, y_hi, core), lane: 8 (over x, y_lo).
Axes of the slice: x: 4, y: 8 (y_hi: 4, y_lo: 2; y = y_hi * 2 + y_lo), z: 8, core: 2. Of those that a mesh axis runs over, the one named last changes fastest.
Arguments:
- waves: float32 [8192, 2048], P('blk'), may hold values from -6 to 6
- pair_bins: int32 [8192, 3, 128], P('blk'), may hold values from 0 to 15
- tile_perm: int32 [64, 64], P('blk'), may hold values from 0 to 63, each once within a row
Outputs:
- gathers: float32 [64, 128, 16, 128], P('blk', 'lane')
Inputs may be any that keep to these rules, and one draw needn't show every extreme that they name: Each row of tile_perm is a permutation of 0 to 64 - 1.
All inputs are finite; a program needn't handle non-finite values.
Results may differ from a plain program's by a relative error of at most 0.0039.
Values may be sent and summed in bfloat16 or wider, within the bound.
No kernel may reach another device: no remote copies, remote signals or barrier semaphores. Data moves between devices by JAX's collectives and lax.ppermute only.
A program may use at most 64 MiB of HBM per device.

v0:
```python
import jax
import jax.numpy as jnp
from jax import lax
from jax.sharding import PartitionSpec as P

LAGS = 64
NBIN = 16
STEPS = 3


def shifted_2(block, axis, distance):
    devices = range(lax.axis_size(axis))
    route = [((i - distance) % len(devices), i) for i in devices]
    return lax.ppermute(block, axis, route)


def on_device(waves, pair_bins, tile_perm):
    node_rows, sample_len = waves.shape
    cycle_size = lax.axis_size("blk")
    lane_count = lax.axis_size("lane")
    lag_dev = LAGS // lane_count
    lag_start = lax.axis_index("lane") * lag_dev
    row_norms = jnp.sqrt(jnp.mean(waves * waves, axis=1, keepdims=True) + 1e-06)
    normed = (waves / row_norms).astype(jnp.bfloat16)
    levels = jnp.arange(NBIN, dtype=jnp.int32)
    forward_sums = jnp.zeros((node_rows, NBIN, lag_dev), jnp.float32)
    reverse_sum = jnp.zeros((node_rows, NBIN, lag_dev), jnp.float32)
    visitor = normed
    for step_index in range(STEPS):
        if step_index > 0:
            visitor = shifted_2(visitor, "blk", 1)
            reverse_sum = shifted_2(reverse_sum, "blk", 1)
        padded = jnp.concatenate([visitor, jnp.zeros((node_rows, LAGS), jnp.bfloat16)], axis=1)
        layers = []
        for lag_index in range(lag_dev):
            shifted = lax.dynamic_slice_in_dim(padded, lag_start + lag_index, sample_len, 1)
            layers.append(
                lax.dot_general(
                    normed, shifted, (((1,), (1,)), ((), ())), preferred_element_type=jnp.float32
                )
            )
        products = jnp.stack(layers, axis=2) / sample_len
        bin_onehot = (pair_bins[:, step_index, :, None] == levels).astype(jnp.float32)
        forward_sums = forward_sums + jnp.einsum(
            "imb,imk->ibk", bin_onehot, products, precision=lax.Precision.HIGHEST
        )
        reverse_sum = reverse_sum + jnp.einsum(
            "imb,imk->mbk", bin_onehot, products, precision=lax.Precision.HIGHEST
        )
    returned = shifted_2(reverse_sum, "blk", -(STEPS - 1))
    joined = jnp.stack([forward_sums, returned], axis=2)
    tile_stack = joined.reshape(cycle_size, node_rows // cycle_size, NBIN, 2, lag_dev)
    chosen = jnp.take(tile_stack, tile_perm[0], axis=0)
    arrived = lax.all_to_all(
        lax.all_to_all(chosen, "blk", split_axis=0, concat_axis=0, tiled=True),
        "lane",
        split_axis=0,
        concat_axis=4,
        tiled=True,
    )
    return arrived.reshape(1, arrived.shape[0] * arrived.shape[1], NBIN, 2 * LAGS)


def solution(mesh):
    placed = (P("blk", None), P("blk", None, None), P("blk", None))
    return jax.shard_map(
        on_device,
        mesh=mesh,
        in_specs=placed,
        out_specs=P("blk", "lane", None, None),
        check_vma=False,
    )
```

profile of v0, /device:TPU:1, one launch (start us, length us, event | category | flops | bytes accessed | tf_op | source)
XLA Modules:
  0.0 131.6 jit_solution(15090788192690491466)
XLA Ops:
  0.0 1.5 %multiply_reduce_fusion = f32[128]{0:T(128)S(1)} fusion(f32[128,2048]{1,0:T(8,128)} %param.3), kind=kLoop, calls=%fused_computation.56 | loop fusion | flops 524160 | bytes 1049088 | tf_op jit(solution)/shard_map/reduce_sum | solution.py:23
  1.7 5.6 %collective-permute-start = (bf16[128,2048]{1,0:T(8,128)(2,1)S(1)}, bf16[128,2048]{1,0:T(8,128)(2,1)}, u32[]{:S(2)}, u32[]{:S(2)}) collective-permute-start(bf16[128,2048]{1,0:T(8,128)(2,1)S(1)} %divide_convert_fusion), channel_id=1, source_target_pairs={{504,0},{0,8},{8,16},{16,24},{24,32},{32,40},{40,48},{48,56},{56,6... | collective-permute-start | bytes 1572872 | tf_op jit(solution)/shard_map/ppermute | solution.py:14
  7.4 0.4 fusion.23
  7.9 0.4 fusion.22
  8.3 0.4 fusion.21
  8.7 0.4 fusion.20
  9.1 0.4 fusion.19
  9.5 0.4 fusion.18
  9.9 0.4 fusion.17
  10.3 0.4 fusion.16
  11.0 1.7 %fusion.125 = f32[128,16,8]{1,2,0:T(8,128)} fusion(f32[128,128,8]{0,2,1:T(8,128)S(1)} %copy.86, s32[128,128]{0,1:T(8,128)S(1)} %copy.77), kind=kOutput, calls=%fused_computation.171 | convolution fusion | flops 25427968 | bytes 655360 | tf_op jit(solution)/shard_map/imb,imk->mbk/dot_general | solution.py:47
  12.8 1.9 %collective-permute-start.2 = (f32[128,16,8]{1,2,0:T(8,128)}, f32[128,16,8]{1,2,0:T(8,128)S(1)}, u32[]{:S(2)}, u32[]{:S(2)}) collective-permute-start(f32[128,16,8]{1,2,0:T(8,128)} %fusion.125), channel_id=1, source_target_pairs={{504,0},{0,8},{8,16},{16,24},{24,32},{32,40},{40,48},{48,56},{56,6... | collective-permute-start | bytes 196616 | tf_op jit(solution)/shard_map/ppermute | solution.py:14
  15.4 0.9 copy.81
  16.3 0.9 copy.78
  17.2 0.9 copy.84
  18.1 1.1 fusion.26
  19.1 1.4 %fusion.15 = f32[128,128,8]{1,0,2:T(8,128)S(1)} fusion(bf16[128,2048]{1,0:T(8,128)(2,1)S(1)} %divide_convert_fusion, s32[]{:T(128)S(6)} %select_n.61, bf16[128,2048]{1,0:T(8,128)(2,1)} %collective-permute-done), kind=kOutput, calls=%fused_computation.35 | convolution fusion | flops 67108864 | bytes 1114116 | tf_op jit(solution)/shard_map/dot_general | solution.py:38
  20.6 1.4 %fusion.14 = f32[128,128,8]{1,0,2:T(8,128)S(1)} fusion(f32[128,128,8]{1,0,2:T(8,128)S(1)} %fusion.15, bf16[128,2048]{1,0:T(8,128)(2,1)S(1)} %divide_convert_fusion, s32[]{:T(128)S(6)} %select_n.62, bf16[128,2048]{1,0:T(8,128)(2,1)} %collective-permute-done), kind=kOutput, calls=%fused_computation.33 | convolution fusion | flops 67108864 | bytes 1114116 | tf_op jit(solution)/shard_map/dot_general | solution.py:38
  22.0 1.4 %fusion.13 = f32[128,128,8]{1,0,2:T(8,128)S(1)} fusion(f32[128,128,8]{1,0,2:T(8,128)S(1)} %fusion.14, bf16[128,2048]{1,0:T(8,128)(2,1)S(1)} %divide_convert_fusion, s32[]{:T(128)S(6)} %select_n.63, bf16[128,2048]{1,0:T(8,128)(2,1)} %collective-permute-done), kind=kOutput, calls=%fused_computation.31 | convolution fusion | flops 67108864 | bytes 1114116 | tf_op jit(solution)/shard_map/dot_general | solution.py:38
  23.5 1.4 %fusion.12 = f32[128,128,8]{1,0,2:T(8,128)S(1)} fusion(f32[128,128,8]{1,0,2:T(8,128)S(1)} %fusion.13, bf16[128,2048]{1,0:T(8,128)(2,1)S(1)} %divide_convert_fusion, s32[]{:T(128)S(6)} %select_n.64, bf16[128,2048]{1,0:T(8,128)(2,1)} %collective-permute-done), kind=kOutput, calls=%fused_computation.29 | convolution fusion | flops 67108864 | bytes 1114116 | tf_op jit(solution)/shard_map/dot_general | solution.py:38
  24.9 1.4 %fusion.11 = f32[128,128,8]{1,0,2:T(8,128)S(1)} fusion(f32[128,128,8]{1,0,2:T(8,128)S(1)} %fusion.12, bf16[128,2048]{1,0:T(8,128)(2,1)S(1)} %divide_convert_fusion, s32[]{:T(128)S(6)} %select_n.65, bf16[128,2048]{1,0:T(8,128)(2,1)} %collective-permute-done), kind=kOutput, calls=%fused_computation.27 | convolution fusion | flops 67108864 | bytes 1114116 | tf_op jit(solution)/shard_map/dot_general | solution.py:38
  26.4 1.4 %fusion.10 = f32[128,128,8]{1,0,2:T(8,128)S(1)} fusion(f32[128,128,8]{1,0,2:T(8,128)S(1)} %fusion.11, bf16[128,2048]{1,0:T(8,128)(2,1)S(1)} %divide_convert_fusion, s32[]{:T(128)S(6)} %select_n.66, bf16[128,2048]{1,0:T(8,128)(2,1)} %collective-permute-done), kind=kOutput, calls=%fused_computation.25 | convolution fusion | flops 67108864 | bytes 1114116 | tf_op jit(solution)/shard_map/dot_general | solution.py:38
  27.8 1.4 %fusion.9 = f32[128,128,8]{1,0,2:T(8,128)S(1)} fusion(f32[128,128,8]{1,0,2:T(8,128)S(1)} %fusion.10, bf16[128,2048]{1,0:T(8,128)(2,1)S(1)} %divide_convert_fusion, s32[]{:T(128)S(6)} %select_n.67, bf16[128,2048]{1,0:T(8,128)(2,1)} %collective-permute-done), kind=kOutput, calls=%fused_computation.23 | convolution fusion | flops 67108864 | bytes 1114116 | tf_op jit(solution)/shard_map/dot_general | solution.py:38
  29.3 1.4 %fusion.8 = f32[128,128,8]{1,0,2:T(8,128)S(1)} fusion(f32[128,128,8]{1,0,2:T(8,128)S(1)} %fusion.9, bf16[128,2048]{1,0:T(8,128)(2,1)S(1)} %divide_convert_fusion, s32[]{:T(128)S(6)} %select_n.68, bf16[128,2048]{1,0:T(8,128)(2,1)} %collective-permute-done), kind=kOutput, calls=%fused_computation.21 | convolution fusion | flops 67108864 | bytes 1114116 | tf_op jit(solution)/shard_map/dot_general | solution.py:38
  31.0 5.8 %collective-permute-start.1 = (bf16[128,2048]{1,0:T(8,128)(2,1)}, bf16[128,2048]{1,0:T(8,128)(2,1)S(1)}, u32[]{:S(2)}, u32[]{:S(2)}) collective-permute-start(bf16[128,2048]{1,0:T(8,128)(2,1)} %collective-permute-done), channel_id=1, source_target_pairs={{504,0},{0,8},{8,16},{16,24},{24,32},{32,40},{40,48},{48,56},{56,6... | collective-permute-start | bytes 1572872 | tf_op jit(solution)/shard_map/ppermute | solution.py:14
  36.9 0.9 convolution_add_fusion
  37.8 2.2 %collective-permute-start.3 = (f32[128,16,8]{1,2,0:T(8,128)S(1)}, f32[128,16,8]{1,2,0:T(8,128)S(1)}, u32[]{:S(2)}, u32[]{:S(2)}) collective-permute-start(f32[128,16,8]{1,2,0:T(8,128)S(1)} %convolution_add_fusion), channel_id=1, source_target_pairs={{504,0},{0,8},{8,16},{16,24},{24,32},{32,40},{40,48},{48,56},{56,6... | collective-permute-start | bytes 196616 | tf_op jit(solution)/shard_map/ppermute | solution.py:14
  40.0 1.1 convolution_add_fusion.2
  41.1 2.2 %collective-permute-done.1 = bf16[128,2048]{1,0:T(8,128)(2,1)S(1)} collective-permute-done((bf16[128,2048]{1,0:T(8,128)(2,1)}, bf16[128,2048]{1,0:T(8,128)(2,1)S(1)}, u32[]{:S(2)}, u32[]{:S(2)}) %collective-permute-start.1) | collective-permute-done | bytes 524320 | tf_op jit(solution)/shard_map/ppermute | solution.py:14
  43.7 0.4 fusion.6
  44.1 0.4 fusion.5
  44.5 0.4 fusion.4
  44.9 0.4 fusion.3
  45.3 0.4 fusion.2
  45.7 0.4 fusion.1
  46.1 0.4 fusion
  46.8 0.9 fusion.126
  47.8 1.1 collective-permute-done.3
  49.0 22.5 %collective-permute-start.4 = (f32[128,16,8]{1,2,0:T(8,128)S(1)}, f32[128,16,8]{1,2,0:T(8,128)S(1)}, u32[]{:S(2)}, u32[]{:S(2)}) collective-permute-start(f32[128,16,8]{1,2,0:T(8,128)S(1)} %add.161), channel_id=1, source_target_pairs={{16,0},{24,8},{32,16},{40,24},{48,32},{56,40},{64,48},{72,56},{80,... | collective-permute-start | bytes 196616 | tf_op jit(solution)/shard_map/ppermute | solution.py:14
  71.5 1.1 convolution_add_fusion.1
  72.6 21.2 %collective-permute-done.4 = f32[128,16,8]{1,2,0:T(8,128)S(1)} collective-permute-done((f32[128,16,8]{1,2,0:T(8,128)S(1)}, f32[128,16,8]{1,2,0:T(8,128)S(1)}, u32[]{:S(2)}, u32[]{:S(2)}) %collective-permute-start.4) | collective-permute-done | bytes 65568 | tf_op jit(solution)/shard_map/ppermute | solution.py:14
  93.9 0.6 gather_fusion
  95.1 22.4 %all_to_all.20 = f32[64,1,512]{2,1,0:T(1,128)S(1)} all-to-all(f32[64,1,512]{2,1,0:T(1,128)S(1)} %reshape.63), channel_id=1, replica_groups=mesh['blk'=64,'lane'=8] {'blk'}, dimensions={0} | all-to-all | bytes 262144 | tf_op jit(solution)/shard_map/all_to_all | solution.py:55
  117.5 0.5 broadcast.56
  118.0 0.9 reduce
  119.8 9.4 %all_to_all.21 = f32[8,1,4096]{2,1,0:T(1,128)S(1)} all-to-all(f32[8,1,4096]{2,1,0:T(1,128)S(1)} %reshape.65), channel_id=1, replica_groups=mesh['blk'=64,'lane'=8] {'lane'}, dimensions={0} | all-to-all | bytes 262144 | tf_op jit(solution)/shard_map/all_to_all | solution.py:54
  129.2 1.0 reduce.1
  130.6 1.0 copy.92
  (40 shorter events, 4.1 us)
Async XLA Ops:
  0.0 1.5 %copy-start = (f32[128,2048]{1,0:T(8,128)S(1)}, f32[128,2048]{1,0:T(8,128)}, u32[]{:S(2)}) copy-start(f32[128,2048]{1,0:T(8,128)} %param.3) | copy-start | bytes 3145732
  1.5 5.8 %copy-start.3 = (s32[128,3,128]{2,0,1:T(8,128)S(1)}, s32[128,3,128]{2,0,1:T(8,128)}, u32[]{:S(2)}) copy-start(s32[128,3,128]{2,0,1:T(8,128)} %param.4) | copy-start | bytes 589828
  1.7 27.6 %copy-start.1 = (bf16[128,2048]{1,0:T(8,128)(2,1)}, bf16[128,2048]{1,0:T(8,128)(2,1)S(1)}, u32[]{:S(2)}) copy-start(bf16[128,2048]{1,0:T(8,128)(2,1)S(1)} %divide_convert_fusion) | copy-start | bytes 1572868
  1.7 17.4 %collective-permute-start = (bf16[128,2048]{1,0:T(8,128)(2,1)S(1)}, bf16[128,2048]{1,0:T(8,128)(2,1)}, u32[]{:S(2)}, u32[]{:S(2)}) collective-permute-start(bf16[128,2048]{1,0:T(8,128)(2,1)S(1)} %divide_convert_fusion), channel_id=1, source_target_pairs={{504,0},{0,8},{8,16},{16,24},{24,32},{32,40},{40,48},{48,56},{56,6... | collective-permute-start | bytes 1572872 | tf_op jit(solution)/shard_map/ppermute | solution.py:14
  10.8 4.1 %copy-start.4 = (s32[1,64]{1,0:T(1,128)S(1)}, s32[1,64]{1,0:T(1,128)}, u32[]{:S(2)}) copy-start(s32[1,64]{1,0:T(1,128)} %param.5) | copy-start | bytes 772
  12.8 24.1 %collective-permute-start.2 = (f32[128,16,8]{1,2,0:T(8,128)}, f32[128,16,8]{1,2,0:T(8,128)S(1)}, u32[]{:S(2)}, u32[]{:S(2)}) collective-permute-start(f32[128,16,8]{1,2,0:T(8,128)} %fusion.125), channel_id=1, source_target_pairs={{504,0},{0,8},{8,16},{16,24},{24,32},{32,40},{40,48},{48,56},{56,6... | collective-permute-start | bytes 196616 | tf_op jit(solution)/shard_map/ppermute | solution.py:14
  31.0 12.2 %collective-permute-start.1 = (bf16[128,2048]{1,0:T(8,128)(2,1)}, bf16[128,2048]{1,0:T(8,128)(2,1)S(1)}, u32[]{:S(2)}, u32[]{:S(2)}) collective-permute-start(bf16[128,2048]{1,0:T(8,128)(2,1)} %collective-permute-done), channel_id=1, source_target_pairs={{504,0},{0,8},{8,16},{16,24},{24,32},{32,40},{40,48},{48,56},{56,6... | collective-permute-start | bytes 1572872 | tf_op jit(solution)/shard_map/ppermute | solution.py:14
  37.8 5.5 %copy-start.2 = (bf16[128,2048]{1,0:T(8,128)(2,1)S(1)}, bf16[128,2048]{1,0:T(8,128)(2,1)}, u32[]{:S(2)}) copy-start(bf16[128,2048]{1,0:T(8,128)(2,1)} %copy-done.1) | copy-start | bytes 1572868
  37.8 11.1 %collective-permute-start.3 = (f32[128,16,8]{1,2,0:T(8,128)S(1)}, f32[128,16,8]{1,2,0:T(8,128)S(1)}, u32[]{:S(2)}, u32[]{:S(2)}) collective-permute-start(f32[128,16,8]{1,2,0:T(8,128)S(1)} %convolution_add_fusion), channel_id=1, source_target_pairs={{504,0},{0,8},{8,16},{16,24},{24,32},{32,40},{40,48},{48,56},{56,6... | collective-permute-start | bytes 196616 | tf_op jit(solution)/shard_map/ppermute | solution.py:14
  49.0 44.8 %collective-permute-start.4 = (f32[128,16,8]{1,2,0:T(8,128)S(1)}, f32[128,16,8]{1,2,0:T(8,128)S(1)}, u32[]{:S(2)}, u32[]{:S(2)}) collective-permute-start(f32[128,16,8]{1,2,0:T(8,128)S(1)} %add.161), channel_id=1, source_target_pairs={{16,0},{24,8},{32,16},{40,24},{48,32},{56,40},{64,48},{72,56},{80,... | collective-permute-start | bytes 196616 | tf_op jit(solution)/shard_map/ppermute | solution.py:14
where the time goes:
time: 132 us
  starting transfers between devices  38.1 us (29%)
  blocking collectives  31.8 us (24%)
  matrix products  24.8 us (19%)
  waiting for transfers between devices  24.5 us (19%)
  local copies, waits for them, and re-layouts  7.48 us (6%)
  other arithmetic  4.38 us (3%)
    ppermute x5, starting transfers between devices, shifted_2(): return lax.ppermute(block, axis, route)  38.1 us
    ppermute x5, waiting for transfers between devices, shifted_2(): return lax.ppermute(block, axis, route)  24.5 us
    all_to_all x1, blocking collectives, on_device(): lax.all_to_all(chosen, 'blk', split_axis=0, concat_axis=0, tiled=True)  22.4 us
    dot_general x24, matrix products, on_device(): lax.dot_general(normed, shifted, (((1,), (1,)), ((), ())), preferred_elem...  18 us
    all_to_all x1, blocking collectives, on_device(): lax.all_to_all(lax.all_to_all(chosen, 'blk', split_axis=0, concat_axis=0,...  9.37 us
    dot_general x3, matrix products, on_device(): jnp.einsum('imb,imk->mbk', bin_onehot, products, precision=lax.Precision....  3.59 us
    dot_general x3, matrix products, on_device(): jnp.einsum('imb,imk->ibk', bin_onehot, products, precision=lax.Precision....  3.19 us
    eq x7, local copies, waits for them, and re-layouts, on_device(): pair_bins[:, step_index, :, None] == levels  2.91 us
  transfers between devices with their start and end apart: 5, of which 3 were waited for; matrix products, arithmetic and copies ran while one was open for 22% of the time, Pallas kernels for 0%

commit v1 on v0

v1 whole, which is shorter than its diff:
```python
import jax
import jax.numpy as jnp
from jax import lax
from jax.experimental import pallas as pl
from jax.experimental.pallas import tpu as pltpu
from jax.sharding import PartitionSpec as P

S = 2048
LAGS = 64
NBIN = 16
STEPS = 3
BLOCK = 128
GROUPS = 8
PAD = S + 128
WIDE = S + 2 * BLOCK
BF = jnp.bfloat16
F32 = jnp.float32
AXES = ("blk", "lane")


def device(z, h, core, x, y):
    return ((z % 8) * 8 + h * 2 + core) * 8 + x * 2 + y


PLACES = [
    (z, h, c, x, y)
    for z in range(8)
    for h in range(4)
    for c in range(2)
    for x in range(4)
    for y in range(2)
]


def beside(z, h, step):
    chip = (z * 4 + h + step) % 32
    return chip // 4, chip % 4


ACROSS = [
    (device(*pos), device(*beside(pos[0], pos[1], 1 if pos[4] else -1), pos[2], pos[3], 1 - pos[4]))
    for pos in PLACES
]
PARTNER = [(device(*pos), device(pos[0], pos[1], 1 - pos[2], pos[3], pos[4])) for pos in PLACES]
TURN = [
    (device(z, h, c, x, y), device(2 * x + y, h, c, z // 2, z % 2)) for z, h, c, x, y in PLACES
]
ROUND = [
    [device(z, h, c, x, y) for y in range(2) for h in range(4) for c in range(2)]
    for z in range(8)
    for x in range(4)
]


def dot(a, b):
    return lax.dot_general(a, b, (((1,), (0,)), ((), ())), preferred_element_type=F32)


def prepare(waves_ref, bins_ref, load_ref, own_ref):
    for r in range(0, BLOCK, 32):
        w = waves_ref[r : r + 32, :]
        norm = jnp.sqrt(jnp.mean(w * w, axis=1, keepdims=True) + 1e-06)
        load_ref[r : r + 32, :S] = (w / norm).astype(BF)
    for s in range(STEPS):
        b = bins_ref[s].astype(F32)
        turned = jnp.transpose(b).astype(BF)
        own_ref[s] = b.astype(BF)
        if s == 0:
            own_ref[STEPS] = turned
        else:
            load_ref[:, S + (s - 1) * BLOCK : S + s * BLOCK] = turned


def toeplitz(place_ref, perm_ref, load_ref, out_ref, pick_ref):
    g = pl.program_id(0)
    tiles = [perm_ref[0, place_ref[1] + 2 * g + own] * 2 for own in range(2)]
    node = [tiles[i % 2] + i // 2 for i in range(4)]

    def chosen(rows, which):
        at = which(lax.broadcasted_iota(jnp.int32, (rows, BLOCK), 0))
        want = jnp.where(at < 2, jnp.where(at == 0, node[0], node[1]), jnp.where(at == 2, node[2], node[3]))
        return (lax.broadcasted_iota(jnp.int32, (rows, BLOCK), 1) == want).astype(BF)

    pick_ref[...] = chosen(64, lambda r: r // NBIN)
    x = dot(chosen(16, lambda r: r % 4), load_ref[:, :S])
    x = jnp.concatenate([x, jnp.zeros((16, PAD - S), F32)], axis=1)
    x = jnp.where(place_ref[0] == 0, pltpu.roll(x, LAGS - 1, 1), x)
    row = lax.broadcasted_iota(jnp.int32, (16, PAD), 0) // 4
    base = x
    for kk in range(1, 4):
        base = jnp.where(row == kk, pltpu.roll(x, PAD - kk, 1), base)
    for q in range(16):
        moved = base if q == 0 else pltpu.roll(base, PAD - 4 * q, 1)
        out_ref[0, q * 16 : (q + 1) * 16, :] = moved[:, :S].astype(BF)


def correlate(place_ref, pick_ref, own_ref, load_ref, far_ref, near_ref, shift_ref, out_ref, sums_ref):
    g = pl.program_id(0)
    rows = GROUPS * 64

    @pl.when(g == 0)
    def _():
        level = (lax.broadcasted_iota(jnp.int32, (rows, BLOCK), 0) % NBIN).astype(F32)
        forward = place_ref[0] == 0
        pick = pick_ref[...]
        tables = (
            jnp.where(forward, own_ref[0], own_ref[3]),
            jnp.where(forward, own_ref[1], near_ref[:, S : S + BLOCK]),
            jnp.where(forward, own_ref[2], far_ref[:, S + BLOCK :]),
        )
        hot = [(dot(pick, t) == level).astype(BF) for t in tables]
        for n in range(0, S, 256):
            at = slice(n, n + 256)
            v = dot(hot[0], load_ref[:, at]) + dot(hot[2], far_ref[:, at]) + dot(hot[1], near_ref[:, at])
            top = v.astype(BF)
            rest = (v - top.astype(F32)).astype(BF)
            sums_ref[:, 0:64, at] = top.reshape(GROUPS, 64, 256)
            sums_ref[:, 64:128, at] = rest.reshape(GROUPS, 64, 256)

    full = lax.dot_general(
        sums_ref[g], shift_ref[0], (((1,), (1,)), ((), ())), preferred_element_type=F32
    )
    c = (full[0:64] + full[64:128]) * (1.0 / S)
    r = lax.broadcasted_iota(jnp.int32, (64, 256), 0) // 16
    k = lax.broadcasted_iota(jnp.int32, (64, 256), 1) % 4
    c = jnp.where(r == k, c, 0.0).astype(BF)
    lag = lax.broadcasted_iota(jnp.int32, (256, 128), 0) // 4
    col = lax.broadcasted_iota(jnp.int32, (256, 128), 1)
    first = (lag == col).astype(BF)
    second = (lag + LAGS == col).astype(BF)
    out = dot(c[0:32], first) + dot(c[32:64], second)
    out_ref[...] = out.astype(BF).reshape(2, NBIN, 128)


def assemble(y_ref, out_ref):
    i = lax.broadcasted_iota(jnp.int32, (128, 256), 0)
    o = lax.broadcasted_iota(jnp.int32, (128, 256), 1)
    same = (i // LAGS) == (o // 128)
    early = jnp.logical_and(same, o % 128 == LAGS - 1 - i % LAGS).astype(BF)
    late = jnp.logical_and(same, o % 128 == LAGS + i % LAGS).astype(BF)
    out = dot(y_ref[0:8].reshape(128, 128), early) + dot(y_ref[8:16].reshape(128, 128), late)
    for q in range(2):
        out_ref[:, q] = out[:, q * 128 : (q + 1) * 128].reshape(8, NBIN, 128)


def whole(shape):
    return pl.BlockSpec(shape, lambda *_: (0,) * len(shape))


SCALAR = pl.BlockSpec(memory_space=pltpu.SMEM)


def limit(mib):
    return pltpu.CompilerParams(vmem_limit_bytes=mib << 20)


def on_device(waves, pair_bins, tile_perm):
    core = lax.axis_index("blk") % 2
    lane = lax.axis_index("lane")
    x, y = lane // 2, lane % 2
    place = jnp.stack([y, x * 16])

    load, own = pl.pallas_call(
        prepare,
        out_shape=(
            jax.ShapeDtypeStruct((BLOCK, WIDE), BF),
            jax.ShapeDtypeStruct((4, BLOCK, BLOCK), BF),
        ),
        compiler_params=limit(16),
        name="prepare",
    )(waves, jnp.transpose(pair_bins, (1, 0, 2)))

    far = lax.ppermute(load, AXES, ACROSS)

    shifts, pick = pl.pallas_call(
        toeplitz,
        grid=(GROUPS,),
        in_specs=[SCALAR, SCALAR, whole((BLOCK, WIDE))],
        out_specs=(
            pl.BlockSpec((1, 256, S), lambda g: (g, 0, 0)),
            pl.BlockSpec((64, BLOCK), lambda g: (g, 0)),
        ),
        out_shape=(
            jax.ShapeDtypeStruct((GROUPS, 256, S), BF),
            jax.ShapeDtypeStruct((GROUPS * 64, BLOCK), BF),
        ),
        compiler_params=limit(16),
        cost_estimate=pl.CostEstimate(flops=2 * 128 * 128 * S, bytes_accessed=GROUPS * 512 * S, transcendentals=0),
        name="toeplitz",
    )(place, tile_perm, load)
    far, shifts, pick = lax.optimization_barrier((far, shifts, pick))

    near = lax.ppermute(jnp.where(core == y, load, far), AXES, PARTNER)

    mine = pl.pallas_call(
        correlate,
        grid=(GROUPS,),
        in_specs=[
            SCALAR,
            whole((GROUPS * 64, BLOCK)),
            whole((4, BLOCK, BLOCK)),
            whole((BLOCK, WIDE)),
            whole((BLOCK, WIDE)),
            whole((BLOCK, WIDE)),
            pl.BlockSpec((1, 256, S), lambda g: (g, 0, 0)),
        ],
        out_specs=pl.BlockSpec((2, NBIN, 128), lambda g: (g, 0, 0)),
        out_shape=jax.ShapeDtypeStruct((16, NBIN, 128), BF),
        scratch_shapes=[pltpu.VMEM((GROUPS, 128, S), BF)],
        compiler_params=limit(32),
        name="correlate",
    )(place, pick, own, load, far, near, shifts)

    mine = lax.all_to_all(mine, AXES, 0, 0, axis_index_groups=ROUND, tiled=True)
    mine = lax.ppermute(mine, AXES, TURN)
    out = pl.pallas_call(
        assemble,
        out_shape=jax.ShapeDtypeStruct((8, 2, NBIN, 128), F32),
        compiler_params=limit(16),
        name="assemble",
    )(mine)
    return out.reshape(1, 16, NBIN, 128)


def solution(mesh):
    placed = (P("blk", None), P("blk", None, None), P("blk", None))
    return jax.shard_map(
        on_device,
        mesh=mesh,
        in_specs=placed,
        out_specs=P("blk", "lane", None, None),
        check_vma=False,
    )
```

time: 132 us -> 65 us (0.49)
  the two profiles are of different devices: /device:TPU:1 before, /device:TPU:4 now
where the time goes in v1:
time: 65 us; the launch traced here: 64.7 us
  starting transfers between devices  22.1 us (34%)
  waiting for transfers between devices  15.1 us (23%)
  Pallas kernels  14.1 us (22%)
  blocking collectives  10.5 us (16%)
  local copies, waits for them, and re-layouts  2.81 us (4%)
    ppermute x1, starting transfers between devices, on_device(): far = lax.ppermute(load, AXES, ACROSS)  13.9 us
    all_to_all x1, blocking collectives, on_device(): mine = lax.all_to_all(mine, AXES, 0, 0, axis_index_groups=ROUND, tiled=True)  10.5 us
    pallas_call x1, Pallas kernels, on_device(): pl.pallas_call(correlate, grid=(GROUPS,), in_specs=[SCALAR, whole((GROUPS...  7.45 us
    ppermute x1, waiting for transfers between devices, on_device(): far = lax.ppermute(load, AXES, ACROSS)  6.91 us
    ppermute x1, starting transfers between devices, on_device(): mine = lax.ppermute(mine, AXES, TURN)  6.28 us
    ppermute x1, waiting for transfers between devices, on_device(): mine = lax.ppermute(mine, AXES, TURN)  6.17 us
    pallas_call x1, Pallas kernels, on_device(): pl.pallas_call(toeplitz, grid=(GROUPS,), in_specs=[SCALAR, SCALAR, whole(...  5.63 us
    unnamed x6, local copies, waits for them, and re-layouts  2.81 us
  transfers between devices with their start and end apart: 3, of which 3 were waited for; matrix products, arithmetic and copies ran while one was open for 0% of the time, Pallas kernels for 9%

profile of v1, /device:TPU:4, one launch (start us, length us, event | category | flops | bytes accessed | tf_op | source)
XLA Modules:
  0.0 64.7 jit_solution(11857093890605763206)
XLA Ops:
  0.0 0.0 copy-start
  0.0 1.2 %copy-done = f32[128,2048]{1,0:T(8,128)S(1)} copy-done((f32[128,2048]{1,0:T(8,128)S(1)}, f32[128,2048]{1,0:T(8,128)}, u32[]{:S(2)}) %copy-start) | copy-done | bytes 1048600
  1.2 0.0 copy-start.1
  1.2 0.9 %copy-done.1 = s32[128,3,128]{2,0,1:T(8,128)S(1)} copy-done((s32[128,3,128]{2,0,1:T(8,128)S(1)}, s32[128,3,128]{2,0,1:T(8,128)}, u32[]{:S(2)}) %copy-start.1) | copy-done | bytes 196632
  2.2 0.2 prepare.1
  2.4 13.9 %collective-permute-start = (bf16[128,2304]{1,0:T(8,128)(2,1)S(1)}, bf16[128,2304]{1,0:T(8,128)(2,1)S(1)}, u32[]{:S(2)}, u32[]{:S(2)}) collective-permute-start(bf16[128,2304]{1,0:T(8,128)(2,1)S(1)} %get-tuple-element.12.load_ref), channel_id=1, source_target_pairs={{0,497},{1,16},{2,499},{3,18},{4,501},{5,20},{6,503},{7,22},{8,505... | collective-permute-start | bytes 1769480 | tf_op jit(solution)/shard_map/ppermute | solution.py:173
  16.2 0.1 pad_add_fusion.place_ref
  16.3 0.0 copy-start.2
  16.3 0.7 %copy-done.2 = s32[1,64]{1,0:T(1,128)S(1)} copy-done((s32[1,64]{1,0:T(1,128)S(1)}, s32[1,64]{1,0:T(1,128)}, u32[]{:S(2)}) %copy-start.2) | copy-done | bytes 280
  17.0 5.6 %toeplitz.1 = (bf16[8,256,2048]{2,1,0:T(8,128)(2,1)S(1)}, bf16[512,128]{1,0:T(8,128)(2,1)S(1)}) custom-call(s32[2]{0:T(128)S(1)} %pad_add_fusion.place_ref, s32[1,64]{1,0:T(1,128)S(1)} %copy-done.2, bf16[128,2304]{1,0:T(8,128)(2,1)S(1)} %get-tuple-element.12.load_ref), custom_call_target="tpu_custom_call" | custom-call | flops 67108864 | bytes 8388608 | tf_op jit(solution)/shard_map/toeplitz/pallas_call | solution.py:175
  22.6 6.9 %collective-permute-done.far_ref = bf16[128,2304]{1,0:T(8,128)(2,1)S(1)} collective-permute-done((bf16[128,2304]{1,0:T(8,128)(2,1)S(1)}, bf16[128,2304]{1,0:T(8,128)(2,1)S(1)}, u32[]{:S(2)}, u32[]{:S(2)}) %collective-permute-start) | collective-permute-done | bytes 589856 | tf_op jit(solution)/shard_map/ppermute | solution.py:173
  29.5 0.1 broadcast_select_fusion
  29.6 1.9 %collective-permute-start.1 = (bf16[128,2304]{1,0:T(8,128)(2,1)S(1)}, bf16[128,2304]{1,0:T(8,128)(2,1)S(1)}, u32[]{:S(2)}, u32[]{:S(2)}) collective-permute-start(bf16[128,2304]{1,0:T(8,128)(2,1)S(1)} %broadcast_select_fusion), channel_id=1, source_target_pairs={{0,8},{1,9},{2,10},{3,11},{4,12},{5,13},{6,14},{7,15},{8,0},{9,1},... | collective-permute-start | bytes 1769480 | tf_op jit(solution)/shard_map/ppermute | solution.py:193
  31.5 2.0 %collective-permute-done.1.near_ref = bf16[128,2304]{1,0:T(8,128)(2,1)S(1)} collective-permute-done((bf16[128,2304]{1,0:T(8,128)(2,1)S(1)}, bf16[128,2304]{1,0:T(8,128)(2,1)S(1)}, u32[]{:S(2)}, u32[]{:S(2)}) %collective-permute-start.1) | collective-permute-done | bytes 589856 | tf_op jit(solution)/shard_map/ppermute | solution.py:193
  33.5 7.5 %correlate.1 = bf16[16,16,128]{2,1,0:T(8,128)(2,1)S(1)} custom-call(s32[2]{0:T(128)S(1)} %pad_add_fusion.place_ref, bf16[512,128]{1,0:T(8,128)(2,1)S(1)} %get-tuple-element.15.pick_ref, bf16[4,128,128]{2,1,0:T(8,128)(2,1)S(1)} %get-tuple-element.16.own_ref, bf16[128,2304]{1,0:T(8,128)(2,1)S(1)} %get-tuple-element.12.load_ref, ...), custom_call_target="tpu_custom_call" | custom-call | tf_op jit(solution)/shard_map/correlate/pallas_call | solution.py:195
  41.0 10.5 %all_to_all.5 = bf16[16,16,128]{2,1,0:T(8,128)(2,1)S(1)} all-to-all(bf16[16,16,128]{2,1,0:T(8,128)(2,1)S(1)} %correlate.1), channel_id=1, replica_groups={{0,8,16,24,32,40,48,56,1,9,17,25,33,41,49,57},{2,10,18,26,34,42,50,58,3..., dimensions={0} | all-to-all | bytes 131072 | tf_op jit(solution)/shard_map/all_to_all | solution.py:214
  51.4 6.3 %collective-permute-start.2 = (bf16[16,16,128]{2,1,0:T(8,128)(2,1)S(1)}, bf16[16,16,128]{2,1,0:T(8,128)(2,1)S(1)}, u32[]{:S(2)}, u32[]{:S(2)}) collective-permute-start(bf16[16,16,128]{2,1,0:T(8,128)(2,1)S(1)} %all_to_all.5), channel_id=1, source_target_pairs={{0,0},{1,64},{2,128},{3,192},{4,256},{5,320},{6,384},{7,448},{8,8}... | collective-permute-start | bytes 196616 | tf_op jit(solution)/shard_map/ppermute | solution.py:215
  57.7 6.2 %collective-permute-done.2.y_ref = bf16[16,16,128]{2,1,0:T(8,128)(2,1)S(1)} collective-permute-done((bf16[16,16,128]{2,1,0:T(8,128)(2,1)S(1)}, bf16[16,16,128]{2,1,0:T(8,128)(2,1)S(1)}, u32[]{:S(2)}, u32[]{:S(2)}) %collective-permute-start.2) | collective-permute-done | bytes 65568 | tf_op jit(solution)/shard_map/ppermute | solution.py:215
  63.9 0.8 %assemble.1 = f32[8,2,16,128]{3,2,1,0:T(8,128)} custom-call(bf16[16,16,128]{2,1,0:T(8,128)(2,1)S(1)} %collective-permute-done.2.y_ref), custom_call_target="tpu_custom_call" | custom-call | tf_op jit(solution)/shard_map/assemble/pallas_call | solution.py:216
Async XLA Ops:
  0.0 1.2 %copy-start = (f32[128,2048]{1,0:T(8,128)S(1)}, f32[128,2048]{1,0:T(8,128)}, u32[]{:S(2)}) copy-start(f32[128,2048]{1,0:T(8,128)} %waves_ref.1) | copy-start | bytes 3145732
  1.2 0.9 %copy-start.1 = (s32[128,3,128]{2,0,1:T(8,128)S(1)}, s32[128,3,128]{2,0,1:T(8,128)}, u32[]{:S(2)}) copy-start(s32[128,3,128]{2,0,1:T(8,128)} %param.4) | copy-start | bytes 589828
  2.4 27.2 %collective-permute-start = (bf16[128,2304]{1,0:T(8,128)(2,1)S(1)}, bf16[128,2304]{1,0:T(8,128)(2,1)S(1)}, u32[]{:S(2)}, u32[]{:S(2)}) collective-permute-start(bf16[128,2304]{1,0:T(8,128)(2,1)S(1)} %get-tuple-element.12.load_ref), channel_id=1, source_target_pairs={{0,497},{1,16},{2,499},{3,18},{4,501},{5,20},{6,503},{7,22},{8,505... | collective-permute-start | bytes 1769480 | tf_op jit(solution)/shard_map/ppermute | solution.py:173
  16.3 0.7 %copy-start.2 = (s32[1,64]{1,0:T(1,128)S(1)}, s32[1,64]{1,0:T(1,128)}, u32[]{:S(2)}) copy-start(s32[1,64]{1,0:T(1,128)} %perm_ref.1) | copy-start | bytes 772
  29.6 3.9 %collective-permute-start.1 = (bf16[128,2304]{1,0:T(8,128)(2,1)S(1)}, bf16[128,2304]{1,0:T(8,128)(2,1)S(1)}, u32[]{:S(2)}, u32[]{:S(2)}) collective-permute-start(bf16[128,2304]{1,0:T(8,128)(2,1)S(1)} %broadcast_select_fusion), channel_id=1, source_target_pairs={{0,8},{1,9},{2,10},{3,11},{4,12},{5,13},{6,14},{7,15},{8,0},{9,1},... | collective-permute-start | bytes 1769480 | tf_op jit(solution)/shard_map/ppermute | solution.py:193
  51.4 12.5 %collective-permute-start.2 = (bf16[16,16,128]{2,1,0:T(8,128)(2,1)S(1)}, bf16[16,16,128]{2,1,0:T(8,128)(2,1)S(1)}, u32[]{:S(2)}, u32[]{:S(2)}) collective-permute-start(bf16[16,16,128]{2,1,0:T(8,128)(2,1)S(1)} %all_to_all.5), channel_id=1, source_target_pairs={{0,0},{1,64},{2,128},{3,192},{4,256},{5,320},{6,384},{7,448},{8,8}... | collective-permute-start | bytes 196616 | tf_op jit(solution)/shard_map/ppermute | solution.py:215

commit v2 on v0

v2 whole, which is shorter than its diff:
```python
import jax
import jax.numpy as jnp
from jax import lax
from jax.experimental import pallas as pl
from jax.experimental.pallas import tpu as pltpu
from jax.sharding import PartitionSpec as P

S = 2048
LAGS = 64
NBIN = 16
STEPS = 3
BLOCK = 128
GROUPS = 16
ROWS = GROUPS * 64
HALF = S // 2
PAD = HALF + 128
WIDE = HALF + 2 * BLOCK
BF = jnp.bfloat16
F32 = jnp.float32
AXES = ("blk", "lane")


def device(z, h, core, x, y):
    return ((z % 8) * 8 + h * 2 + core) * 8 + x * 2 + y


PLACES = [
    (z, h, c, x, y)
    for z in range(8)
    for h in range(4)
    for c in range(2)
    for x in range(4)
    for y in range(2)
]


def beside(z, h, step):
    chip = (z * 4 + h + step) % 32
    return chip // 4, chip % 4


ACROSS = [
    (device(*pos), device(*beside(pos[0], pos[1], 1 if pos[4] else -1), pos[2], pos[3], 1 - pos[4]))
    for pos in PLACES
]
PARTNER = [(device(*pos), device(pos[0], pos[1], 1 - pos[2], pos[3], pos[4])) for pos in PLACES]


def ring(a, b, n):
    return min((a - b) % n, (b - a) % n)


OFFSETS = 0x72016534


def owner_z(z, x, y):
    near = ((x + 4 - (z >> 1)) & 3) * 2 + ((y + z) & 1)
    return (z + ((OFFSETS >> (4 * near)) & 7)) & 7


TURN = [
    (device(z, h, c, x, y), device(owner_z(z, x, y), h, c, z // 2, z % 2))
    for z, h, c, x, y in PLACES
]
ROUND = [
    [
        device(z, h, c, 2 * pair + x, y)
        for x in range(2)
        for y in range(2)
        for h in range(4)
        for c in range(2)
    ]
    for z in range(8)
    for pair in range(2)
]


def dot(a, b):
    return lax.dot_general(a, b, (((1,), (0,)), ((), ())), preferred_element_type=F32)


def prepare(lane_ref, waves_ref, bins_ref, load_ref, full_ref, own_ref):
    low = (lane_ref[0] & 2) == 0
    for r in range(0, BLOCK, 32):
        w = waves_ref[r : r + 32, :]
        norm = jnp.sqrt(jnp.mean(w * w, axis=1, keepdims=True) + 1e-06)
        w = w / norm
        full_ref[r : r + 32, :] = w.astype(BF)
        load_ref[r : r + 32, :HALF] = jnp.where(low, w[:, :HALF], w[:, HALF:]).astype(BF)
    for s in range(STEPS):
        b = bins_ref[s].astype(F32)
        turned = jnp.transpose(b).astype(BF)
        own_ref[s] = b.astype(BF)
        if s == 0:
            own_ref[STEPS] = turned
        else:
            load_ref[:, HALF + (s - 1) * BLOCK : HALF + s * BLOCK] = turned


def one_hot(pick, table):
    level = (lax.broadcasted_iota(jnp.int32, (ROWS, BLOCK), 0) % NBIN).astype(F32)
    return (dot(pick, table) == level).astype(BF)


def early(lane_ref, blk_ref, perm_ref, full_ref, load_ref, own_ref, out_ref, pick_ref, base_ref, rows_ref):
    def chosen(g, rows, which):
        at = which(lax.broadcasted_iota(jnp.int32, (rows, BLOCK), 0))
        first = 8 * owner_z(blk_ref[0] >> 3, ((lane_ref[0] >> 2) << 1) + g // 8, g // 4 % 2) + 2 * (g % 4)
        tiles = [perm_ref[0, first + own] * 2 for own in range(2)]
        node = [tiles[i % 2] + i // 2 for i in range(4)]
        want = jnp.where(at < 2, jnp.where(at == 0, node[0], node[1]), jnp.where(at == 2, node[2], node[3]))
        return (lax.broadcasted_iota(jnp.int32, (rows, BLOCK), 1) == want).astype(BF)

    for g in range(GROUPS):
        pick_ref[g * 64 : (g + 1) * 64, :] = chosen(g, 64, lambda r: r // NBIN)
    few = jnp.concatenate([chosen(g, 16, lambda r: r % 4) for g in range(GROUPS)], axis=0)
    x = dot(few, full_ref[...])
    x = jnp.concatenate([x, jnp.zeros((GROUPS * 16, 128), F32)], axis=1)
    x = jnp.where((lane_ref[0] & 1) == 0, pltpu.roll(x, LAGS - 1, 1), x)
    x = jnp.where((lane_ref[0] & 2) == 0, x[:, :PAD], x[:, HALF:])
    row = lax.broadcasted_iota(jnp.int32, (GROUPS * 16, PAD), 0) // 4 % 4
    base = x
    for kk in range(1, 4):
        base = jnp.where(row == kk, pltpu.roll(x, PAD - kk, 1), base)
    rows_ref[...] = base.astype(BF).reshape(GROUPS, 16, PAD)

    @pl.loop(0, GROUPS)
    def _(g):
        some = rows_ref[g]
        for q in range(16):
            moved = some if q == 0 else pltpu.roll(some, PAD - 4 * q, 1)
            out_ref[g, q * 16 : (q + 1) * 16, :] = moved[:, :HALF]

    hot = one_hot(pick_ref[...], jnp.where((lane_ref[0] & 1) == 0, own_ref[0], own_ref[3]))
    for n in range(0, HALF, 256):
        base_ref[:, n : n + 256] = dot(hot, load_ref[:, n : n + 256])


def middle(lane_ref, pick_ref, own_ref, far_ref, base_ref, out_ref):
    hot = one_hot(pick_ref[...], jnp.where((lane_ref[0] & 1) == 0, own_ref[2], far_ref[:, HALF + BLOCK :]))
    for n in range(0, HALF, 256):
        out_ref[:, n : n + 256] = base_ref[:, n : n + 256] + dot(hot, far_ref[:, n : n + 256])


def correlate(lane_ref, pick_ref, own_ref, near_ref, base_ref, shift_ref, out_ref, sums_ref, flat_ref):
    hot = one_hot(pick_ref[...], jnp.where((lane_ref[0] & 1) == 0, own_ref[1], near_ref[:, HALF : HALF + BLOCK]))
    for n in range(0, HALF, 256):
        v = base_ref[:, n : n + 256] + dot(hot, near_ref[:, n : n + 256])
        top = v.astype(BF)
        rest = (v - top.astype(F32)).astype(BF)
        sums_ref[:, 0:64, n : n + 256] = top.reshape(GROUPS, 64, 256)
        sums_ref[:, 64:128, n : n + 256] = rest.reshape(GROUPS, 64, 256)
    r = lax.broadcasted_iota(jnp.int32, (64, 256), 0) // NBIN
    k = lax.broadcasted_iota(jnp.int32, (64, 256), 1) % 4
    for g in range(GROUPS):
        c = lax.dot_general(
            sums_ref[g], shift_ref[g], (((1,), (1,)), ((), ())), preferred_element_type=F32
        )
        c = jnp.where(r == k, (c[0:64] + c[64:128]) * (1.0 / S), 0.0).astype(BF)
        flat_ref[0, g * 32 : (g + 1) * 32, :] = c[0:32]
        flat_ref[1, g * 32 : (g + 1) * 32, :] = c[32:64]
    lag = lax.broadcasted_iota(jnp.int32, (256, 128), 0) // 4
    col = lax.broadcasted_iota(jnp.int32, (256, 128), 1)
    out = dot(flat_ref[0], (lag == col).astype(BF)) + dot(flat_ref[1], (lag + LAGS == col).astype(BF))
    out_ref[...] = out.astype(BF).reshape(2 * GROUPS, NBIN, 128)


def assemble(y_ref, out_ref):
    i = lax.broadcasted_iota(jnp.int32, (128, 256), 0)
    o = lax.broadcasted_iota(jnp.int32, (128, 256), 1)
    same = (i // LAGS) == (o // 128)
    early = jnp.logical_and(same, o % 128 == LAGS - 1 - i % LAGS).astype(BF)
    late = jnp.logical_and(same, o % 128 == LAGS + i % LAGS).astype(BF)
    out = dot(y_ref[0:8].reshape(128, 128), early) + dot(y_ref[8:16].reshape(128, 128), late)
    for q in range(2):
        out_ref[:, q] = out[:, q * 128 : (q + 1) * 128].reshape(8, NBIN, 128)


SCALAR = pl.BlockSpec(memory_space=pltpu.SMEM)
VMEM = pl.BlockSpec(memory_space=pltpu.VMEM)


def call(kernel, out, specs, scratch=(), flops=0):
    return pl.pallas_call(
        kernel,
        out_shape=[jax.ShapeDtypeStruct(shape, kind) for shape, kind in out],
        in_specs=specs,
        out_specs=[VMEM] * len(out),
        scratch_shapes=scratch,
        compiler_params=pltpu.CompilerParams(vmem_limit_bytes=20 << 20),
        cost_estimate=pl.CostEstimate(flops=flops, bytes_accessed=flops // 400, transcendentals=0),
        name=kernel.__name__,
    )


def on_device(waves, pair_bins, tile_perm):
    blk, lane = lax.axis_index("blk"), lax.axis_index("lane")
    core, y = blk % 2, lane % 2
    here = lane.reshape(1)

    load, full, own = call(
        prepare,
        [((BLOCK, WIDE), BF), ((BLOCK, S), BF), ((4, BLOCK, BLOCK), BF)],
        [SCALAR, VMEM, VMEM],
    )(here, waves, jnp.transpose(pair_bins, (1, 0, 2)))

    far = lax.ppermute(load, AXES, ACROSS)
    shifts, pick, base = call(
        early,
        [((GROUPS, 256, HALF), BF), ((ROWS, BLOCK), BF), ((ROWS, HALF), F32)],
        [SCALAR] * 3 + [VMEM] * 3,
        [pltpu.VMEM((GROUPS, 16, PAD), BF)],
        flops=1 << 32,
    )(here, blk.reshape(1), tile_perm, full, load, own)
    far, shifts, pick, base = lax.optimization_barrier((far, shifts, pick, base))

    near = lax.ppermute(jnp.where(core == y, load, far), AXES, PARTNER)
    (base,) = call(middle, [((ROWS, HALF), F32)], [SCALAR] + [VMEM] * 4, flops=1 << 29)(
        here, pick, own, far, base
    )
    near, base = lax.optimization_barrier((near, base))
    (mine,) = call(
        correlate,
        [((2 * GROUPS, NBIN, 128), BF)],
        [SCALAR] + [VMEM] * 5,
        [pltpu.VMEM((GROUPS, 128, HALF), BF), pltpu.VMEM((2, ROWS // 2, 256), BF)],
        flops=1 << 31,
    )(here, pick, own, near, base, shifts)

    mine = lax.all_to_all(mine, AXES, 0, 0, axis_index_groups=ROUND, tiled=True).astype(F32)
    mine = (mine[:16] + mine[16:]).astype(BF)
    mine = lax.ppermute(mine, AXES, TURN)
    (out,) = call(assemble, [((8, 2, NBIN, 128), F32)], [VMEM])(mine)
    return out.reshape(1, 16, NBIN, 128)


def solution(mesh):
    placed = (P("blk", None), P("blk", None, None), P("blk", None))
    return jax.shard_map(
        on_device,
        mesh=mesh,
        in_specs=placed,
        out_specs=P("blk", "lane", None, None),
        check_vma=False,
    )
```

time: 132 us -> 56 us (0.42)
  the two profiles are of different devices: /device:TPU:1 before, /device:TPU:7 now
where the time goes in v2:
time: 56 us; the launch traced here: 55.7 us
  starting transfers between devices  19.2 us (34%)
  blocking collectives  12.1 us (22%)
  Pallas kernels  11.5 us (21%)
  waiting for transfers between devices  9.86 us (18%)
  local copies, waits for them, and re-layouts  2.8 us (5%)
    ppermute x1, starting transfers between devices, on_device(): far = lax.ppermute(load, AXES, ACROSS)  13.6 us
    all_to_all x1, blocking collectives, on_device(): lax.all_to_all(mine, AXES, 0, 0, axis_index_groups=ROUND, tiled=True)  12.1 us
    ppermute x1, waiting for transfers between devices, on_device(): mine = lax.ppermute(mine, AXES, TURN)  8.76 us
    pallas_call x1, Pallas kernels, on_device(): call(early, [((GROUPS, 256, HALF), BF), ((ROWS, BLOCK), BF), ((ROWS, HALF...  5.99 us
    pallas_call x1, Pallas kernels, on_device(): call(correlate, [((2 * GROUPS, NBIN, 128), BF)], [SCALAR] + [VMEM] * 5, [...  3.57 us
    ppermute x1, starting transfers between devices, on_device(): near = lax.ppermute(jnp.where(core == y, load, far), AXES, PARTNER)  3.16 us
    unnamed x6, local copies, waits for them, and re-layouts  2.8 us
    ppermute x1, starting transfers between devices, on_device(): mine = lax.ppermute(mine, AXES, TURN)  2.52 us
  transfers between devices with their start and end apart: 3, of which 3 were waited for; matrix products, arithmetic and copies ran while one was open for 0% of the time, Pallas kernels for 12%

profile of v2, /device:TPU:7, one launch (start us, length us, event | category | flops | bytes accessed | tf_op | source)
XLA Modules:
  0.0 55.7 jit_solution(2304350594670495356)
XLA Ops:
  0.0 0.0 copy-start
  0.0 1.2 %copy-done = f32[128,2048]{1,0:T(8,128)S(1)} copy-done((f32[128,2048]{1,0:T(8,128)S(1)}, f32[128,2048]{1,0:T(8,128)}, u32[]{:S(2)}) %copy-start) | copy-done | bytes 1048600
  1.2 0.0 copy-start.1
  1.2 0.9 %copy-done.1 = s32[128,3,128]{2,0,1:T(8,128)S(1)} copy-done((s32[128,3,128]{2,0,1:T(8,128)S(1)}, s32[128,3,128]{2,0,1:T(8,128)}, u32[]{:S(2)}) %copy-start.1) | copy-done | bytes 196632
  2.2 0.2 prepare.1
  2.4 13.6 %collective-permute-start = (bf16[128,1280]{1,0:T(8,128)(2,1)S(1)}, bf16[128,1280]{1,0:T(8,128)(2,1)S(1)}, u32[]{:S(2)}, u32[]{:S(2)}) collective-permute-start(bf16[128,1280]{1,0:T(8,128)(2,1)S(1)} %get-tuple-element.17.load_ref), channel_id=1, source_target_pairs={{0,497},{1,16},{2,499},{3,18},{4,501},{5,20},{6,503},{7,22},{8,505... | collective-permute-start | bytes 983048 | tf_op jit(solution)/shard_map/ppermute | solution.py:207
  16.0 0.0 copy-start.2
  16.0 0.6 %copy-done.2 = s32[1,64]{1,0:T(1,128)S(1)} copy-done((s32[1,64]{1,0:T(1,128)S(1)}, s32[1,64]{1,0:T(1,128)}, u32[]{:S(2)}) %copy-start.2) | copy-done | bytes 280
  16.7 6.0 %early.1 = (bf16[16,256,1024]{2,1,0:T(8,128)(2,1)S(1)}, bf16[1024,128]{1,0:T(8,128)(2,1)S(1)}, f32[1024,1024]{1,0:T(8,128)S(1)}) custom-call(s32[1]{0:T(128)} %bitcast.lane_ref, s32[1]{0:T(128)} %bitcast.2.blk_ref, s32[1,64]{1,0:T(1,128)S(1)} %copy-done.2, bf16[128,2048]{1,0:T(8,128)(2,1)S(1)} %get-tuple-element.18.full_ref, ...), custom_call_target="tpu_custom_call" | custom-call | flops 4294967296 | bytes 10737418 | tf_op jit(solution)/shard_map/early/pallas_call | solution.py:208
  22.6 0.7 %collective-permute-done.far_ref = bf16[128,1280]{1,0:T(8,128)(2,1)S(1)} collective-permute-done((bf16[128,1280]{1,0:T(8,128)(2,1)S(1)}, bf16[128,1280]{1,0:T(8,128)(2,1)S(1)}, u32[]{:S(2)}, u32[]{:S(2)}) %collective-permute-start) | collective-permute-done | bytes 327712 | tf_op jit(solution)/shard_map/ppermute | solution.py:207
  23.4 3.2 %collective-permute-start.1 = (bf16[128,1280]{1,0:T(8,128)(2,1)S(1)}, bf16[128,1280]{1,0:T(8,128)(2,1)S(1)}, u32[]{:S(2)}, u32[]{:S(2)}) collective-permute-start(bf16[128,1280]{1,0:T(8,128)(2,1)S(1)} %broadcast_select_fusion), channel_id=1, source_target_pairs={{0,8},{1,9},{2,10},{3,11},{4,12},{5,13},{6,14},{7,15},{8,0},{9,1},... | collective-permute-start | bytes 983048 | tf_op jit(solution)/shard_map/ppermute | solution.py:217
  26.6 0.8 %middle.1.base_ref = f32[1024,1024]{1,0:T(8,128)S(1)} custom-call(s32[1]{0:T(128)} %bitcast.lane_ref, bf16[1024,128]{1,0:T(8,128)(2,1)S(1)} %get-tuple-element.23.pick_ref, bf16[4,128,128]{2,1,0:T(8,128)(2,1)S(1)} %get-tuple-element.19.own_ref, bf16[128,1280]{1,0:T(8,128)(2,1)S(1)} %collective-permute-done.far_ref, f32[1024,1024]{1,0:T(8,128)S(1)} %get-tuple-element.25.base_ref), custom_call_target="tpu_custom_call" | custom-call | flops 536870912 | bytes 1342177 | tf_op jit(solution)/shard_map/middle/pallas_call | solution.py:218
  27.4 0.4 collective-permute-done.1.near_ref
  27.8 3.6 %correlate.1 = bf16[32,16,128]{2,1,0:T(8,128)(2,1)S(1)} custom-call(s32[1]{0:T(128)} %bitcast.lane_ref, bf16[1024,128]{1,0:T(8,128)(2,1)S(1)} %get-tuple-element.23.pick_ref, bf16[4,128,128]{2,1,0:T(8,128)(2,1)S(1)} %get-tuple-element.19.own_ref, bf16[128,1280]{1,0:T(8,128)(2,1)S(1)} %collective-permute-done.1.near_ref, f32[1024,1024]{1,0:T(8,128)S(1)} %middle.1.base_ref, ...), custom_call_target="tpu_custom_call" | custom-call | flops 2147483648 | bytes 5368709 | tf_op jit(solution)/shard_map/correlate/pallas_call | solution.py:222
  31.4 12.1 %all_to_all.5 = bf16[32,16,128]{2,1,0:T(8,128)(2,1)S(1)} all-to-all(bf16[32,16,128]{2,1,0:T(8,128)(2,1)S(1)} %correlate.1), channel_id=1, replica_groups={{0,8,16,24,32,40,48,56,1,9,17,25,33,41,49,57,2,10,18,26,34,42,50,58,3,1..., dimensions={0} | all-to-all | bytes 262144 | tf_op jit(solution)/shard_map/all_to_all | solution.py:230
  43.6 2.5 %collective-permute-start.2 = (bf16[16,16,128]{2,1,0:T(8,128)(2,1)S(1)}, bf16[16,16,128]{2,1,0:T(8,128)(2,1)S(1)}, u32[]{:S(2)}, u32[]{:S(2)}) collective-permute-start(bf16[16,16,128]{2,1,0:T(8,128)(2,1)S(1)} %fusion), channel_id=1, source_target_pairs={{0,256},{1,192},{2,320},{3,384},{4,64},{5,0},{6,128},{7,448},{8,26... | collective-permute-start | bytes 196616 | tf_op jit(solution)/shard_map/ppermute | solution.py:232
  46.1 8.8 %collective-permute-done.2.y_ref = bf16[16,16,128]{2,1,0:T(8,128)(2,1)S(1)} collective-permute-done((bf16[16,16,128]{2,1,0:T(8,128)(2,1)S(1)}, bf16[16,16,128]{2,1,0:T(8,128)(2,1)S(1)}, u32[]{:S(2)}, u32[]{:S(2)}) %collective-permute-start.2) | collective-permute-done | bytes 65568 | tf_op jit(solution)/shard_map/ppermute | solution.py:232
  54.8 0.8 %assemble.1 = f32[8,2,16,128]{3,2,1,0:T(8,128)} custom-call(bf16[16,16,128]{2,1,0:T(8,128)(2,1)S(1)} %collective-permute-done.2.y_ref), custom_call_target="tpu_custom_call" | custom-call | tf_op jit(solution)/shard_map/assemble/pallas_call | solution.py:233
  (3 shorter events, 0.1 us)
Async XLA Ops:
  0.0 1.2 %copy-start = (f32[128,2048]{1,0:T(8,128)S(1)}, f32[128,2048]{1,0:T(8,128)}, u32[]{:S(2)}) copy-start(f32[128,2048]{1,0:T(8,128)} %waves_ref.1) | copy-start | bytes 3145732
  1.2 0.9 %copy-start.1 = (s32[128,3,128]{2,0,1:T(8,128)S(1)}, s32[128,3,128]{2,0,1:T(8,128)}, u32[]{:S(2)}) copy-start(s32[128,3,128]{2,0,1:T(8,128)} %param.4) | copy-start | bytes 589828
  2.4 21.0 %collective-permute-start = (bf16[128,1280]{1,0:T(8,128)(2,1)S(1)}, bf16[128,1280]{1,0:T(8,128)(2,1)S(1)}, u32[]{:S(2)}, u32[]{:S(2)}) collective-permute-start(bf16[128,1280]{1,0:T(8,128)(2,1)S(1)} %get-tuple-element.17.load_ref), channel_id=1, source_target_pairs={{0,497},{1,16},{2,499},{3,18},{4,501},{5,20},{6,503},{7,22},{8,505... | collective-permute-start | bytes 983048 | tf_op jit(solution)/shard_map/ppermute | solution.py:207
  16.0 0.7 %copy-start.2 = (s32[1,64]{1,0:T(1,128)S(1)}, s32[1,64]{1,0:T(1,128)}, u32[]{:S(2)}) copy-start(s32[1,64]{1,0:T(1,128)} %perm_ref.1) | copy-start | bytes 772
  23.4 4.4 %collective-permute-start.1 = (bf16[128,1280]{1,0:T(8,128)(2,1)S(1)}, bf16[128,1280]{1,0:T(8,128)(2,1)S(1)}, u32[]{:S(2)}, u32[]{:S(2)}) collective-permute-start(bf16[128,1280]{1,0:T(8,128)(2,1)S(1)} %broadcast_select_fusion), channel_id=1, source_target_pairs={{0,8},{1,9},{2,10},{3,11},{4,12},{5,13},{6,14},{7,15},{8,0},{9,1},... | collective-permute-start | bytes 983048 | tf_op jit(solution)/shard_map/ppermute | solution.py:217
  43.6 11.3 %collective-permute-start.2 = (bf16[16,16,128]{2,1,0:T(8,128)(2,1)S(1)}, bf16[16,16,128]{2,1,0:T(8,128)(2,1)S(1)}, u32[]{:S(2)}, u32[]{:S(2)}) collective-permute-start(bf16[16,16,128]{2,1,0:T(8,128)(2,1)S(1)} %fusion), channel_id=1, source_target_pairs={{0,256},{1,192},{2,320},{3,384},{4,64},{5,0},{6,128},{7,448},{8,26... | collective-permute-start | bytes 196616 | tf_op jit(solution)/shard_map/ppermute | solution.py:232

commit v3 on v2

--- a/solution.py
+++ b/solution.py
@@ -79,14 +79,25 @@
     return lax.dot_general(a, b, (((1,), (0,)), ((), ())), preferred_element_type=F32)
 
 
-def prepare(lane_ref, waves_ref, bins_ref, load_ref, full_ref, own_ref):
+def prepare(lane_ref, waves_hbm, bins_hbm, load_ref, full_ref, own_ref, waves_ref, bins_ref, sems):
+    parts = range(0, BLOCK, 32)
+    copies = [
+        pltpu.make_async_copy(waves_hbm.at[r : r + 32], waves_ref.at[r : r + 32], sems.at[i])
+        for i, r in enumerate(parts)
+    ]
+    bins_copy = pltpu.make_async_copy(bins_hbm, bins_ref, sems.at[4])
+    for copy in copies:
+        copy.start()
+    bins_copy.start()
     low = (lane_ref[0] & 2) == 0
-    for r in range(0, BLOCK, 32):
+    for i, r in enumerate(parts):
+        copies[i].wait()
         w = waves_ref[r : r + 32, :]
         norm = jnp.sqrt(jnp.mean(w * w, axis=1, keepdims=True) + 1e-06)
         w = w / norm
         full_ref[r : r + 32, :] = w.astype(BF)
         load_ref[r : r + 32, :HALF] = jnp.where(low, w[:, :HALF], w[:, HALF:]).astype(BF)
+    bins_copy.wait()
     for s in range(STEPS):
         b = bins_ref[s].astype(F32)
         turned = jnp.transpose(b).astype(BF)
@@ -177,17 +188,18 @@
 
 
 SCALAR = pl.BlockSpec(memory_space=pltpu.SMEM)
+HBM = pl.BlockSpec(memory_space=pltpu.HBM)
 VMEM = pl.BlockSpec(memory_space=pltpu.VMEM)
 
 
-def call(kernel, out, specs, scratch=(), flops=0):
+def call(kernel, out, specs, scratch=(), flops=0, mib=20):
     return pl.pallas_call(
         kernel,
         out_shape=[jax.ShapeDtypeStruct(shape, kind) for shape, kind in out],
         in_specs=specs,
         out_specs=[VMEM] * len(out),
         scratch_shapes=scratch,
-        compiler_params=pltpu.CompilerParams(vmem_limit_bytes=20 << 20),
+        compiler_params=pltpu.CompilerParams(vmem_limit_bytes=mib << 20),
         cost_estimate=pl.CostEstimate(flops=flops, bytes_accessed=flops // 400, transcendentals=0),
         name=kernel.__name__,
     )
@@ -201,7 +213,9 @@
     load, full, own = call(
         prepare,
         [((BLOCK, WIDE), BF), ((BLOCK, S), BF), ((4, BLOCK, BLOCK), BF)],
-        [SCALAR, VMEM, VMEM],
+        [SCALAR, HBM, HBM],
+        [pltpu.VMEM((BLOCK, S), F32), pltpu.VMEM((STEPS, BLOCK, BLOCK), jnp.int32), pltpu.SemaphoreType.DMA((5,))],
+        mib=52,
     )(here, waves, jnp.transpose(pair_bins, (1, 0, 2)))
 
     far = lax.ppermute(load, AXES, ACROSS)
@@ -214,7 +228,8 @@
     )(here, blk.reshape(1), tile_perm, full, load, own)
     far, shifts, pick, base = lax.optimization_barrier((far, shifts, pick, base))
 
-    near = lax.ppermute(jnp.where(core == y, load, far), AXES, PARTNER)
+    used = HALF + BLOCK
+    near = lax.ppermute(jnp.where(core == y, load[:, :used], far[:, :used]), AXES, PARTNER)
     (base,) = call(middle, [((ROWS, HALF), F32)], [SCALAR] + [VMEM] * 4, flops=1 << 29)(
         here, pick, own, far, base
     )

time: 56 us -> 56.1 us (level)
  Pallas kernels: 11.5 us -> 12.9 us
  local copies, waits for them, and re-layouts: 2.8 us -> 1.58 us
    pallas_call x1, Pallas kernels: 0.23 us -> 1.65 us  [on_device(): call(prepare, [((BLOCK, WIDE), BF), ((BLOCK, S), BF), ((4, BLOCK, BLOCK),...]
    unnamed x6 -> x4, local copies, waits for them, and re-layouts: 2.8 us -> 1.58 us
where the time goes in v3:
time: 56.1 us; the launch traced here: 55.8 us
  starting transfers between devices  19.2 us (34%)
  Pallas kernels  12.9 us (23%)
  blocking collectives  12.1 us (22%)
  waiting for transfers between devices  9.82 us (18%)
  local copies, waits for them, and re-layouts  1.58 us (3%)
    ppermute x1, starting transfers between devices, on_device(): far = lax.ppermute(load, AXES, ACROSS)  13.6 us
    all_to_all x1, blocking collectives, on_device(): lax.all_to_all(mine, AXES, 0, 0, axis_index_groups=ROUND, tiled=True)  12.1 us
    ppermute x1, waiting for transfers between devices, on_device(): mine = lax.ppermute(mine, AXES, TURN)  8.77 us
    pallas_call x1, Pallas kernels, on_device(): call(early, [((GROUPS, 256, HALF), BF), ((ROWS, BLOCK), BF), ((ROWS, HALF...  6 us
    pallas_call x1, Pallas kernels, on_device(): call(correlate, [((2 * GROUPS, NBIN, 128), BF)], [SCALAR] + [VMEM] * 5, [...  3.57 us
    ppermute x1, starting transfers between devices, on_device(): lax.ppermute(jnp.where(core == y, load[:, :used], far[:, :used]), AXES, P...  3.16 us
    ppermute x1, starting transfers between devices, on_device(): mine = lax.ppermute(mine, AXES, TURN)  2.51 us
    pallas_call x1, Pallas kernels, on_device(): call(prepare, [((BLOCK, WIDE), BF), ((BLOCK, S), BF), ((4, BLOCK, BLOCK),...  1.65 us
  transfers between devices with their start and end apart: 3, of which 3 were waited for; matrix products, arithmetic and copies ran while one was open for 0% of the time, Pallas kernels for 12%

profile of v3, /device:TPU:7, one launch (start us, length us, event | category | flops | bytes accessed | tf_op | source)
XLA Modules:
  0.0 55.8 jit_solution(5330400505396859146)
XLA Ops:
  0.0 0.0 copy-start
  0.0 0.9 %copy-done = s32[128,3,128]{2,0,1:T(8,128)S(1)} copy-done((s32[128,3,128]{2,0,1:T(8,128)S(1)}, s32[128,3,128]{2,0,1:T(8,128)}, u32[]{:S(2)}) %copy-start) | copy-done | bytes 196632
  0.9 1.7 %prepare.1 = (bf16[128,1280]{1,0:T(8,128)(2,1)S(1)}, bf16[128,2048]{1,0:T(8,128)(2,1)S(1)}, bf16[4,128,128]{2,1,0:T(8,128)(2,1)S(1)}) custom-call(s32[1]{0:T(128)} %bitcast.lane_ref, f32[128,2048]{1,0:T(8,128)} %waves_hbm.1, s32[3,128,128]{2,1,0:T(8,128)S(1)} %bitcast.4), custom_call_target="tpu_custom_call" | custom-call | tf_op jit(solution)/shard_map/prepare/pallas_call | solution.py:213
  2.6 13.6 %collective-permute-start = (bf16[128,1280]{1,0:T(8,128)(2,1)S(1)}, bf16[128,1280]{1,0:T(8,128)(2,1)S(1)}, u32[]{:S(2)}, u32[]{:S(2)}) collective-permute-start(bf16[128,1280]{1,0:T(8,128)(2,1)S(1)} %get-tuple-element.17.load_ref), channel_id=1, source_target_pairs={{0,497},{1,16},{2,499},{3,18},{4,501},{5,20},{6,503},{7,22},{8,505... | collective-permute-start | bytes 983048 | tf_op jit(solution)/shard_map/ppermute | solution.py:221
  16.2 0.0 copy-start.1
  16.2 0.6 %copy-done.1 = s32[1,64]{1,0:T(1,128)S(1)} copy-done((s32[1,64]{1,0:T(1,128)S(1)}, s32[1,64]{1,0:T(1,128)}, u32[]{:S(2)}) %copy-start.1) | copy-done | bytes 280
  16.9 6.0 %early.1 = (bf16[16,256,1024]{2,1,0:T(8,128)(2,1)S(1)}, bf16[1024,128]{1,0:T(8,128)(2,1)S(1)}, f32[1024,1024]{1,0:T(8,128)S(1)}) custom-call(s32[1]{0:T(128)} %bitcast.lane_ref, s32[1]{0:T(128)} %bitcast.2.blk_ref, s32[1,64]{1,0:T(1,128)S(1)} %copy-done.1, bf16[128,2048]{1,0:T(8,128)(2,1)S(1)} %get-tuple-element.18.full_ref, ...), custom_call_target="tpu_custom_call" | custom-call | flops 4294967296 | bytes 10737418 | tf_op jit(solution)/shard_map/early/pallas_call | solution.py:222
  22.8 0.7 %collective-permute-done.far_ref = bf16[128,1280]{1,0:T(8,128)(2,1)S(1)} collective-permute-done((bf16[128,1280]{1,0:T(8,128)(2,1)S(1)}, bf16[128,1280]{1,0:T(8,128)(2,1)S(1)}, u32[]{:S(2)}, u32[]{:S(2)}) %collective-permute-start) | collective-permute-done | bytes 327712 | tf_op jit(solution)/shard_map/ppermute | solution.py:221
  23.6 3.2 %collective-permute-start.1 = (bf16[128,1152]{1,0:T(8,128)(2,1)S(1)}, bf16[128,1152]{1,0:T(8,128)(2,1)S(1)}, u32[]{:S(2)}, u32[]{:S(2)}) collective-permute-start(bf16[128,1152]{1,0:T(8,128)(2,1)S(1)} %slice_select_fusion), channel_id=1, source_target_pairs={{0,8},{1,9},{2,10},{3,11},{4,12},{5,13},{6,14},{7,15},{8,0},{9,1},... | collective-permute-start | bytes 884744 | tf_op jit(solution)/shard_map/ppermute | solution.py:232
  26.8 0.8 %middle.1.base_ref = f32[1024,1024]{1,0:T(8,128)S(1)} custom-call(s32[1]{0:T(128)} %bitcast.lane_ref, bf16[1024,128]{1,0:T(8,128)(2,1)S(1)} %get-tuple-element.23.pick_ref, bf16[4,128,128]{2,1,0:T(8,128)(2,1)S(1)} %get-tuple-element.19.own_ref, bf16[128,1280]{1,0:T(8,128)(2,1)S(1)} %collective-permute-done.far_ref, f32[1024,1024]{1,0:T(8,128)S(1)} %get-tuple-element.25.base_ref), custom_call_target="tpu_custom_call" | custom-call | flops 536870912 | bytes 1342177 | tf_op jit(solution)/shard_map/middle/pallas_call | solution.py:233
  27.6 0.3 collective-permute-done.1.near_ref
  28.0 3.6 %correlate.1 = bf16[32,16,128]{2,1,0:T(8,128)(2,1)S(1)} custom-call(s32[1]{0:T(128)} %bitcast.lane_ref, bf16[1024,128]{1,0:T(8,128)(2,1)S(1)} %get-tuple-element.23.pick_ref, bf16[4,128,128]{2,1,0:T(8,128)(2,1)S(1)} %get-tuple-element.19.own_ref, bf16[128,1152]{1,0:T(8,128)(2,1)S(1)} %collective-permute-done.1.near_ref, f32[1024,1024]{1,0:T(8,128)S(1)} %middle.1.base_ref, ...), custom_call_target="tpu_custom_call" | custom-call | flops 2147483648 | bytes 5368709 | tf_op jit(solution)/shard_map/correlate/pallas_call | solution.py:237
  31.5 12.1 %all_to_all.5 = bf16[32,16,128]{2,1,0:T(8,128)(2,1)S(1)} all-to-all(bf16[32,16,128]{2,1,0:T(8,128)(2,1)S(1)} %correlate.1), channel_id=1, replica_groups={{0,8,16,24,32,40,48,56,1,9,17,25,33,41,49,57,2,10,18,26,34,42,50,58,3,1..., dimensions={0} | all-to-all | bytes 262144 | tf_op jit(solution)/shard_map/all_to_all | solution.py:245
  43.7 2.5 %collective-permute-start.2 = (bf16[16,16,128]{2,1,0:T(8,128)(2,1)S(1)}, bf16[16,16,128]{2,1,0:T(8,128)(2,1)S(1)}, u32[]{:S(2)}, u32[]{:S(2)}) collective-permute-start(bf16[16,16,128]{2,1,0:T(8,128)(2,1)S(1)} %fusion), channel_id=1, source_target_pairs={{0,256},{1,192},{2,320},{3,384},{4,64},{5,0},{6,128},{7,448},{8,26... | collective-permute-start | bytes 196616 | tf_op jit(solution)/shard_map/ppermute | solution.py:247
  46.2 8.8 %collective-permute-done.2.y_ref = bf16[16,16,128]{2,1,0:T(8,128)(2,1)S(1)} collective-permute-done((bf16[16,16,128]{2,1,0:T(8,128)(2,1)S(1)}, bf16[16,16,128]{2,1,0:T(8,128)(2,1)S(1)}, u32[]{:S(2)}, u32[]{:S(2)}) %collective-permute-start.2) | collective-permute-done | bytes 65568 | tf_op jit(solution)/shard_map/ppermute | solution.py:247
  55.0 0.8 %assemble.1 = f32[8,2,16,128]{3,2,1,0:T(8,128)} custom-call(bf16[16,16,128]{2,1,0:T(8,128)(2,1)S(1)} %collective-permute-done.2.y_ref), custom_call_target="tpu_custom_call" | custom-call | tf_op jit(solution)/shard_map/assemble/pallas_call | solution.py:248
  (3 shorter events, 0.1 us)
Async XLA Ops:
  0.0 0.9 %copy-start = (s32[128,3,128]{2,0,1:T(8,128)S(1)}, s32[128,3,128]{2,0,1:T(8,128)}, u32[]{:S(2)}) copy-start(s32[128,3,128]{2,0,1:T(8,128)} %param.4) | copy-start | bytes 589828
  2.6 21.0 %collective-permute-start = (bf16[128,1280]{1,0:T(8,128)(2,1)S(1)}, bf16[128,1280]{1,0:T(8,128)(2,1)S(1)}, u32[]{:S(2)}, u32[]{:S(2)}) collective-permute-start(bf16[128,1280]{1,0:T(8,128)(2,1)S(1)} %get-tuple-element.17.load_ref), channel_id=1, source_target_pairs={{0,497},{1,16},{2,499},{3,18},{4,501},{5,20},{6,503},{7,22},{8,505... | collective-permute-start | bytes 983048 | tf_op jit(solution)/shard_map/ppermute | solution.py:221
  16.2 0.7 %copy-start.1 = (s32[1,64]{1,0:T(1,128)S(1)}, s32[1,64]{1,0:T(1,128)}, u32[]{:S(2)}) copy-start(s32[1,64]{1,0:T(1,128)} %perm_ref.1) | copy-start | bytes 772
  23.6 4.4 %collective-permute-start.1 = (bf16[128,1152]{1,0:T(8,128)(2,1)S(1)}, bf16[128,1152]{1,0:T(8,128)(2,1)S(1)}, u32[]{:S(2)}, u32[]{:S(2)}) collective-permute-start(bf16[128,1152]{1,0:T(8,128)(2,1)S(1)} %slice_select_fusion), channel_id=1, source_target_pairs={{0,8},{1,9},{2,10},{3,11},{4,12},{5,13},{6,14},{7,15},{8,0},{9,1},... | collective-permute-start | bytes 884744 | tf_op jit(solution)/shard_map/ppermute | solution.py:232
  43.7 11.3 %collective-permute-start.2 = (bf16[16,16,128]{2,1,0:T(8,128)(2,1)S(1)}, bf16[16,16,128]{2,1,0:T(8,128)(2,1)S(1)}, u32[]{:S(2)}, u32[]{:S(2)}) collective-permute-start(bf16[16,16,128]{2,1,0:T(8,128)(2,1)S(1)} %fusion), channel_id=1, source_target_pairs={{0,256},{1,192},{2,320},{3,384},{4,64},{5,0},{6,128},{7,448},{8,26... | collective-permute-start | bytes 196616 | tf_op jit(solution)/shard_map/ppermute | solution.py:247
